TPU v7x, 512 devices: a whole 4x8x8 slice. The times are simulated.
512 devices in a mesh: stn: 16 (over z, core), chan: 32 (over y, x).
Axes of the slice: x: 4, y: 8, z: 8, core: 2. Of those that a mesh axis runs over, the one named last changes fastest.
Arguments:
- voltages: bfloat16 [256, 2048, 512], P('stn', 'chan'), may hold values from -6 to 6
- block_facet: int32 [32, 16, 2048, 1], P('chan', 'stn'), may hold values from 0 to 15; in each aligned block of 2048 rows (0 to 2047, 2048 to 4095, ..., all dimensions but the last counted through in order) at most 192 rows name the same one
- block_tile: int32 [32, 16, 2048], P('chan', 'stn'), may hold values from 0 to 15
- vis_offset: int32 [32, 16, 2048, 128], P('chan', 'stn'), may hold values from 0 to 624
- kernel_taps: bfloat16 [2, 8], replicated, may hold values from 0.19921875 to 1
Outputs:
- image: float32 [2, 2048, 128], P(None, ('stn', 'chan'))
Inputs may be any that keep to these rules, and one draw needn't show every extreme that they name: `block_facet`: among the blocks of one device (one index of the first two dimensions) at most 192 name one facet; in every draw some facet is named by exactly 192 of some device's blocks.
All inputs are finite; a program needn't handle non-finite values.
Results may differ from a plain program's by a relative error of at most 0.0041.
Values may be sent and summed in bfloat16 or wider, within the bound.
A program may use at most 64 MiB of HBM per device.

v0:
```python
import math
import jax
import jax.numpy as jnp
from jax import lax
from jax.sharding import PartitionSpec as P

VB = 128
TILE = 32
KT = 8
TS = 4
TT = 16
OFFS = 25


def kernel_rows(offsets, taps_row):
    cell_ids = jnp.arange(TILE, dtype=jnp.int32)
    distance = cell_ids[None, :, None] - offsets[:, None, :]
    weights_sum = jnp.zeros(distance.shape, jnp.float32)
    for tap_index in range(KT):
        weights_sum = weights_sum + jnp.where(
            distance == tap_index, taps_row[tap_index].astype(jnp.float32), jnp.float32(0.0)
        )
    return weights_sum.astype(jnp.bfloat16)


def block_tiles(values, offsets, kernel_taps):
    along_u = kernel_rows(offsets // OFFS, kernel_taps[0])
    along_v = kernel_rows(offsets % OFFS, kernel_taps[1])
    weighted = (
        values[:, :, None, :].astype(jnp.float32) * along_v[:, None, :, :].astype(jnp.float32)
    ).astype(jnp.bfloat16)
    weighted = weighted.reshape(values.shape[0], 2 * TILE, values.shape[2])
    return jnp.einsum("nux,nwx->nuw", along_u, weighted, preferred_element_type=jnp.float32)


def grid_blocks(values, offsets, target_ids, kernel_taps, segments):
    slot_count = values.shape[0]
    group_size = math.gcd(slot_count, 256)
    tile_width = 2 * TILE * TILE
    segment_ids = jnp.arange(segments, dtype=jnp.int32)

    def accumulate(grids, turn_index):
        first_row = turn_index * group_size
        part_values = lax.dynamic_slice_in_dim(values, first_row, group_size, 0)
        part_offsets = lax.dynamic_slice_in_dim(offsets, first_row, group_size, 0)
        part_targets = lax.dynamic_slice_in_dim(target_ids, first_row, group_size, 0)
        tile_sums = block_tiles(part_values, part_offsets, kernel_taps).reshape(
            group_size, tile_width
        )
        placing = (segment_ids[:, None] == part_targets[None, :]).astype(jnp.float32)
        grids = grids + jnp.dot(
            placing, tile_sums, precision=lax.Precision.HIGHEST, preferred_element_type=jnp.float32
        )
        return (grids, None)

    start_grids = jnp.zeros((segments, tile_width), jnp.float32)
    grids, leftover = lax.scan(accumulate, start_grids, jnp.arange(slot_count // group_size))
    return grids


def facet_grid(tile_grid):
    shaped = tile_grid.reshape(TS, TS, TILE, 2, TILE)
    return jnp.transpose(shaped, (3, 0, 2, 1, 4)).reshape(2, TS * TILE, TS * TILE)


def dft_tables(side):
    index_ids = jnp.arange(side, dtype=jnp.int32)
    phases = index_ids[:, None] * index_ids[None, :] % side
    angles = phases.astype(jnp.float32) * (2.0 * math.pi / side)
    return (jnp.cos(angles), jnp.sin(angles))


def column_pass(grid, cosine, sine):
    high = lax.Precision.HIGHEST
    real_cols = jnp.dot(grid[0], cosine, precision=high) + jnp.dot(grid[1], sine, precision=high)
    imag_cols = jnp.dot(grid[1], cosine, precision=high) - jnp.dot(grid[0], sine, precision=high)
    return (real_cols, imag_cols)


def row_pass(real_cols, imag_cols, cosine_rows, sine_rows):
    high = lax.Precision.HIGHEST
    real_rows = jnp.dot(cosine_rows, real_cols, precision=high) + jnp.dot(
        sine_rows, imag_cols, precision=high
    )
    imag_rows = jnp.dot(cosine_rows, imag_cols, precision=high) - jnp.dot(
        sine_rows, real_cols, precision=high
    )
    return (real_rows, imag_rows)


def body(voltages, block_facet, block_tile, vis_offset, kernel_taps):
    facets = lax.axis_size("stn")
    chan_count = lax.axis_size("chan")
    panels = lax.all_to_all(voltages, "stn", split_axis=1, concat_axis=0, tiled=True)
    stations = panels.shape[0]
    local_channels = panels.shape[1]
    samples = panels.shape[2] // 2
    swapped = jnp.concatenate([panels[:, :, samples:], -panels[:, :, :samples]], axis=2)
    stacked = jnp.concatenate([panels, swapped], axis=0)
    products = jnp.einsum("aks,jks->kaj", stacked, panels, preferred_element_type=jnp.float32)
    station_ids = jnp.arange(stations, dtype=jnp.int32)
    off_diagonal = (station_ids[:, None] != station_ids[None, :]).astype(jnp.float32)
    scale = 1.0 / math.sqrt(samples)
    real_vis = (products[:, :stations, :] * scale * off_diagonal).astype(jnp.bfloat16)
    imag_vis = (products[:, stations:, :] * scale * off_diagonal).astype(jnp.bfloat16)
    block_values = jnp.stack([real_vis.reshape(-1, VB), imag_vis.reshape(-1, VB)], axis=1)
    block_count = block_values.shape[0]
    offsets = vis_offset.reshape(block_count, VB)
    tile_ids = block_tile.reshape(block_count)
    facet_ids = block_facet.reshape(block_count)
    capacity = 3 * block_count // (2 * facets)
    facet_range = jnp.arange(facets, dtype=jnp.int32)
    member = (facet_ids[:, None] == facet_range[None, :]).astype(jnp.int32)
    earlier = jnp.cumsum(member, axis=0) - member
    position = jnp.sum(earlier * member, axis=1)
    slot_ids = facet_ids * capacity + position
    send_values = jnp.zeros((facets * capacity, 2, VB), jnp.bfloat16).at[slot_ids].set(block_values)
    send_offsets = jnp.zeros((facets * capacity, VB), jnp.int32).at[slot_ids].set(offsets)
    send_tiles = jnp.zeros((facets * capacity,), jnp.int32).at[slot_ids].set(tile_ids)
    got_values, got_offsets, got_tiles = (
        lax.all_to_all(send_values, "stn", split_axis=0, concat_axis=0, tiled=True),
        lax.all_to_all(send_offsets, "stn", split_axis=0, concat_axis=0, tiled=True),
        lax.all_to_all(send_tiles, "stn", split_axis=0, concat_axis=0, tiled=True),
    )
    tile_grid = grid_blocks(got_values, got_offsets, got_tiles, kernel_taps, TT)
    grid = facet_grid(tile_grid)
    side = grid.shape[1]
    row_count = side // chan_count
    channels_all = local_channels * facets * chan_count
    norm_factor = 1.0 / math.sqrt(channels_all * stations * stations * KT * KT / facets)
    cosine, sine = dft_tables(side)
    summed = lax.psum(grid, "chan")
    real_cols, imag_cols = column_pass(summed, cosine, sine)
    first_row = lax.axis_index("chan") * row_count
    cosine_rows = lax.dynamic_slice_in_dim(cosine, first_row, row_count, 0)
    sine_rows = lax.dynamic_slice_in_dim(sine, first_row, row_count, 0)
    real_rows, imag_rows = row_pass(real_cols, imag_cols, cosine_rows, sine_rows)
    image = jnp.stack([real_rows, imag_rows], axis=0) * norm_factor
    return image


def solution(mesh):
    placed = (
        P("stn", "chan", None),
        P("chan", "stn", None, None),
        P("chan", "stn", None),
        P("chan", "stn", None, None),
        P(),
    )
    return jax.shard_map(
        body, mesh=mesh, in_specs=placed, out_specs=P(None, ("stn", "chan"), None), check_vma=False
    )
```

profile of v0, /device:TPU:2, one launch (start us, length us, event | category | flops | bytes accessed | tf_op | source)
XLA Modules:
  0.0 876.2 jit_solution(455187938880387183)
XLA Ops:
  7.3 4.5 reduce-window.6
  14.1 8.2 scatter_custom_fusion
  23.0 10.4 %all-to-all-start = ((s32[16,192,1]{1,2,0:T(1,128)}), s32[16,192,1]{1,2,0:T(1,128)S(1)}, u32[]{:S(2)}, u32[]{:S(2)}) async-start(s32[16,192,1]{1,2,0:T(1,128)} %all_to_all.43), calls=%async_computation | async-start | bytes 32768 | tf_op jit(solution)/shard_map/all_to_all | solution.py:123
  36.2 4.9 all-to-all-done
  41.1 3.7 all-to-all-start.2
  44.7 6.8 scatter_custom_fusion.1
  51.6 19.8 %all-to-all-done.2 = bf16[16,64,512]{2,0,1:T(8,128)(2,1)S(1)} async-done(((bf16[16,64,512]{2,0,1:T(8,128)(2,1)}), bf16[16,64,512]{2,0,1:T(8,128)(2,1)S(1)}, u32[]{:S(2)}, u32[]{:S(2)}) %all-to-all-start.2) | async-done | bytes 1048608 | tf_op jit(solution)/shard_map/all_to_all | solution.py:94
  71.3 4.8 all-to-all-start.1
  84.7 185.7 %scatter_fusion = bf16[3072,2,128]{2,1,0:T(2,128)(2,1)} fusion(bf16[3072,2,128]{2,1,0:T(2,128)(2,1)} %broadcast_in_dim.128, s32[2048]{0:T(1024)S(1)} %bitcast.146, bf16[2048,2,128]{2,1,0:T(2,128)(2,1)S(1)} %pad_maximum_fusion), kind=kCustom, calls=%fused_computation.2 | custom fusion | bytes 3153920 | tf_op jit(solution)/shard_map/scatter | solution.py:117
  270.4 7.3 all-to-all-start.3
  278.0 37.6 %all-to-all-done.3 = bf16[3072,2,128]{2,1,0:T(2,128)(2,1)} async-done(((bf16[3072,2,128]{2,1,0:T(2,128)(2,1)}), bf16[3072,2,128]{2,1,0:T(2,128)(2,1)}, u32[]{:S(2)}, u32[]{:S(2)}) %all-to-all-start.3) | async-done | bytes 1572896 | tf_op jit(solution)/shard_map/all_to_all | solution.py:121
  315.6 394.3 %while.13 = (s32[]{:T(128)}, f32[16,2048]{1,0:T(8,128)S(1)}, s32[12]{0:T(128)S(1)}, s32[3072]{0:T(1024)S(1)}, s32[3072,128]{1,0:T(8,128)}, /*index=5*/bf16[2,8]{...) while((s32[]{:T(128)}, f32[16,2048]{1,0:T(8,128)S(1)}, ...), condition=%wide.region_7.8_spmd.clone, body=%wide.region_6.7_spmd.clone.sunk | while | flops 293081088 | bytes 26742172 | solution.py:57
  323.7 3.2 fusion.127
  336.1 7.6 fusion.128
  343.7 3.5 copy.26
  356.5 3.2 fusion.127
  368.9 7.6 fusion.128
  376.6 3.5 copy.26
  389.4 3.2 fusion.127
  401.8 7.6 fusion.128
  409.4 3.5 copy.26
  422.2 3.2 fusion.127
  434.6 7.6 fusion.128
  442.3 3.5 copy.26
  455.1 3.2 fusion.127
  467.5 7.6 fusion.128
  475.1 3.5 copy.26
  487.9 3.2 fusion.127
  500.3 7.6 fusion.128
  507.9 3.5 copy.26
  520.8 3.2 fusion.127
  533.2 7.6 fusion.128
  540.8 3.5 copy.26
  553.6 3.2 fusion.127
  566.0 7.6 fusion.128
  573.6 3.5 copy.26
  586.4 3.2 fusion.127
  598.9 7.6 fusion.128
  606.5 3.5 copy.26
  619.3 3.2 fusion.127
  631.7 7.6 fusion.128
  639.3 3.5 copy.26
  664.5 7.6 fusion.128
  672.2 3.5 copy.26
  685.0 3.2 fusion.127
  697.4 7.6 fusion.128
  705.0 3.5 copy.26
  712.2 150.7 %all-reduce.2.cloned.1.call-done = f32[2,128,128]{2,1,0:T(8,128)} async-done(((f32[2,128,128]{2,1,0:T(8,128)}), f32[2,128,128]{2,1,0:T(8,128)}) %all-reduce.2.cloned.1.call-update) | async-done | bytes 131088 | tf_op jit(solution)/shard_map/psum | solution.py:132
  (127 shorter events, 120.5 us)
Async XLA Ops:
  6.5 38.2 %copy-start = (s32[1,1,2048,128]{3,2,1,0:T(8,128)S(1)}, s32[1,1,2048,128]{3,2,1,0:T(8,128)}, u32[]{:S(2)}) copy-start(s32[1,1,2048,128]{3,2,1,0:T(8,128)} %param.10) | copy-start | bytes 3145732
  23.0 18.1 %all-to-all-start = ((s32[16,192,1]{1,2,0:T(1,128)}), s32[16,192,1]{1,2,0:T(1,128)S(1)}, u32[]{:S(2)}, u32[]{:S(2)}) async-start(s32[16,192,1]{1,2,0:T(1,128)} %all_to_all.43), calls=%async_computation | async-start | bytes 32768 | tf_op jit(solution)/shard_map/all_to_all | solution.py:123
  41.1 30.3 %all-to-all-start.2 = ((bf16[16,64,512]{2,0,1:T(8,128)(2,1)}), bf16[16,64,512]{2,0,1:T(8,128)(2,1)S(1)}, u32[]{:S(2)}, u32[]{:S(2)}) async-start(bf16[16,64,512]{2,0,1:T(8,128)(2,1)} %copy.16), calls=%async_computation.2 | async-start | bytes 2097152 | tf_op jit(solution)/shard_map/all_to_all | solution.py:94
  71.3 199.0 %all-to-all-start.1 = ((s32[16,192,128]{2,1,0:T(8,128)}), s32[16,192,128]{2,1,0:T(8,128)}, u32[]{:S(2)}, u32[]{:S(2)}) async-start(s32[16,192,128]{2,1,0:T(8,128)} %bitcast.8), calls=%async_computation.1 | async-start | bytes 3145728 | tf_op jit(solution)/shard_map/all_to_all | solution.py:122
  82.5 233.0 %copy-start.1 = (bf16[2,8]{1,0:T(2,128)(2,1)S(1)}, bf16[2,8]{1,0:T(2,128)(2,1)}, u32[]{:S(2)}) copy-start(bf16[2,8]{1,0:T(2,128)(2,1)} %param.11) | copy-start | bytes 100
  270.4 45.2 %all-to-all-start.3 = ((bf16[3072,2,128]{2,1,0:T(2,128)(2,1)}), bf16[3072,2,128]{2,1,0:T(2,128)(2,1)}, u32[]{:S(2)}, u32[]{:S(2)}) async-start(bf16[3072,2,128]{2,1,0:T(2,128)(2,1)} %scatter_fusion), calls=%async_computation.3 | async-start | bytes 3145728 | tf_op jit(solution)/shard_map/all_to_all | solution.py:121
  277.6 585.3 %all-reduce.2.cloned.1.call-start = ((), (), s32[]{:S(2)}) async-start(), calls=%async_computation.4 | async-start | bytes 262144 | tf_op jit(solution)/shard_map/psum | solution.py:132
Sparse Core Ops, SparseCore 0:
  711.7 151.1 all-reduce.1
where the time goes:
time: 881 us; the launch traced here: 876 us
  local copies, waits for them, and re-layouts  271 us (31%)
  waiting for transfers between devices  213 us (24%)
  loops' own time  128 us (15%)
  other arithmetic  114 us (13%)
  matrix products  111 us (13%)
  starting transfers between devices  26.4 us (3%)
  between operations  13.6 us (2%)
    scatter x1, local copies, waits for them, and re-layouts, body(): jnp.zeros((facets * capacity, 2, VB), jnp.bfloat16).at[slot_ids]  186 us
    psum x1, waiting for transfers between devices, body(): summed = lax.psum(grid, 'chan')  151 us
    another operation x1, loops' own time, grid_blocks(): lax.scan(accumulate, start_grids, jnp.arange(slot_count // group_size))  128 us
    dot_general x12, matrix products, block_tiles(): jnp.einsum('nux,nwx->nuw', along_u, weighted, preferred_element_type=jnp....  91.5 us
    dot_general x12, local copies, waits for them, and re-layouts, block_tiles(): jnp.einsum('nux,nwx->nuw', along_u, weighted, preferred_element_type=jnp....  42.5 us
    convert_element_type x12, other arithmetic, block_tiles(): along_v[:, None, :, :].astype(jnp.float32)  38.9 us
    convert_element_type x12, other arithmetic, block_tiles(): weighted = (values[:, :, None, :].astype(jnp.float32) * along_v[:, None,...  38.3 us
    all_to_all x1, waiting for transfers between devices, body(): lax.all_to_all(send_values, 'stn', split_axis=0, concat_axis=0, tiled=True)  37.6 us
  transfers between devices with their start and end apart: 5, of which 4 were waited for; matrix products, arithmetic and copies ran while one was open for 23% of the time, Pallas kernels for 0%

commit v1 on v0

--- a/solution.py
+++ b/solution.py
@@ -129,7 +129,7 @@
     channels_all = local_channels * facets * chan_count
     norm_factor = 1.0 / math.sqrt(channels_all * stations * stations * KT * KT / facets)
     cosine, sine = dft_tables(side)
-    summed = lax.psum(grid, "chan")
+    summed = jnp.sum(lax.all_gather(grid, "chan"), axis=0)
     real_cols, imag_cols = column_pass(summed, cosine, sine)
     first_row = lax.axis_index("chan") * row_count
     cosine_rows = lax.dynamic_slice_in_dim(cosine, first_row, row_count, 0)

time: 881 us -> 815 us (0.925)
  the two profiles are of different devices: /device:TPU:2 before, /device:TPU:8 now
where the time goes in v1:
time: 815 us; the launch traced here: 811 us
  local copies, waits for them, and re-layouts  271 us (33%)
  waiting for transfers between devices  148 us (18%)
  loops' own time  128 us (16%)
  other arithmetic  116 us (14%)
  matrix products  107 us (13%)
  starting transfers between devices  26.8 us (3%)
  between operations  13.6 us (2%)
    scatter x1, local copies, waits for them, and re-layouts, body(): jnp.zeros((facets * capacity, 2, VB), jnp.bfloat16).at[slot_ids]  186 us
    another operation x1, loops' own time, grid_blocks(): lax.scan(accumulate, start_grids, jnp.arange(slot_count // group_size))  128 us
    dot_general x12, matrix products, block_tiles(): jnp.einsum('nux,nwx->nuw', along_u, weighted, preferred_element_type=jnp....  91.5 us
    all_gather x1, waiting for transfers between devices, body(): summed = jnp.sum(lax.all_gather(grid, 'chan'), axis=0)  85.6 us
    dot_general x12, local copies, waits for them, and re-layouts, block_tiles(): jnp.einsum('nux,nwx->nuw', along_u, weighted, preferred_element_type=jnp....  42.5 us
    convert_element_type x12, other arithmetic, block_tiles(): along_v[:, None, :, :].astype(jnp.float32)  38.9 us
    convert_element_type x12, other arithmetic, block_tiles(): weighted = (values[:, :, None, :].astype(jnp.float32) * along_v[:, None,...  38.3 us
    all_to_all x1, waiting for transfers between devices, body(): lax.all_to_all(send_values, 'stn', split_axis=0, concat_axis=0, tiled=True)  37.6 us
  transfers between devices with their start and end apart: 5, of which 4 were waited for; matrix products, arithmetic and copies ran while one was open for 25% of the time, Pallas kernels for 0%

profile of v1, /device:TPU:8, one launch (start us, length us, event | category | flops | bytes accessed | tf_op | source)
XLA Modules:
  0.0 810.6 jit_solution(1468969592821285502)
XLA Ops:
  7.3 4.5 reduce-window.6
  14.1 8.2 %scatter_custom_fusion = s32[3072]{0:T(1024)S(1)} fusion(s32[2048]{0:T(1024)S(1)} %bitcast.144, s32[2048]{0:T(1024)} %bitcast.149, s32[]{:T(128)} %constant.120.clone.1), kind=kCustom, calls=%fused_computation.113 | custom fusion | bytes 12800 | tf_op jit(solution)/shard_map/scatter | solution.py:119
  23.0 10.4 %all-to-all-start = ((s32[16,192,1]{1,2,0:T(1,128)}), s32[16,192,1]{1,2,0:T(1,128)S(1)}, u32[]{:S(2)}, u32[]{:S(2)}) async-start(s32[16,192,1]{1,2,0:T(1,128)} %all_to_all.43), calls=%async_computation | async-start | bytes 32768 | tf_op jit(solution)/shard_map/all_to_all | solution.py:123
  36.2 4.9 all-to-all-done
  41.1 3.7 all-to-all-start.2
  44.7 6.8 scatter_custom_fusion.1
  51.6 19.8 %all-to-all-done.2 = bf16[16,64,512]{2,0,1:T(8,128)(2,1)S(1)} async-done(((bf16[16,64,512]{2,0,1:T(8,128)(2,1)}), bf16[16,64,512]{2,0,1:T(8,128)(2,1)S(1)}, u32[]{:S(2)}, u32[]{:S(2)}) %all-to-all-start.2) | async-done | bytes 1048608 | tf_op jit(solution)/shard_map/all_to_all | solution.py:94
  71.3 4.8 all-to-all-start.1
  84.7 185.6 %scatter_fusion = bf16[3072,2,128]{2,1,0:T(2,128)(2,1)} fusion(bf16[3072,2,128]{2,1,0:T(2,128)(2,1)} %broadcast_in_dim.128, s32[2048]{0:T(1024)S(1)} %bitcast.146, bf16[2048,2,128]{2,1,0:T(2,128)(2,1)S(1)} %pad_maximum_fusion), kind=kCustom, calls=%fused_computation.2 | custom fusion | bytes 3153920 | tf_op jit(solution)/shard_map/scatter | solution.py:117
  270.3 7.8 all-to-all-start.3
  278.5 37.6 %all-to-all-done.3 = bf16[3072,2,128]{2,1,0:T(2,128)(2,1)} async-done(((bf16[3072,2,128]{2,1,0:T(2,128)(2,1)}), bf16[3072,2,128]{2,1,0:T(2,128)(2,1)}, u32[]{:S(2)}, u32[]{:S(2)}) %all-to-all-start.3) | async-done | bytes 1572896 | tf_op jit(solution)/shard_map/all_to_all | solution.py:121
  316.0 394.4 %while.13 = (s32[]{:T(128)}, f32[16,2048]{1,0:T(8,128)S(1)}, s32[12]{0:T(128)S(1)}, s32[3072]{0:T(1024)S(1)}, s32[3072,128]{1,0:T(8,128)}, /*index=5*/bf16[2,8]{...) while((s32[]{:T(128)}, f32[16,2048]{1,0:T(8,128)S(1)}, ...), condition=%wide.region_7.8_spmd.clone, body=%wide.region_6.7_spmd.clone.sunk | while | flops 293081088 | bytes 26742172 | solution.py:57
  324.1 3.2 fusion.127
  336.5 7.6 fusion.128
  344.2 3.5 copy.26
  357.0 3.2 fusion.127
  369.4 7.6 fusion.128
  377.0 3.5 copy.26
  389.8 3.2 fusion.127
  402.2 7.6 fusion.128
  409.9 3.5 copy.26
  422.7 3.2 fusion.127
  435.1 7.6 fusion.128
  442.7 3.5 copy.26
  455.5 3.2 fusion.127
  467.9 7.6 fusion.128
  475.6 3.5 copy.26
  488.4 3.2 fusion.127
  500.8 7.6 fusion.128
  508.4 3.5 copy.26
  521.2 3.2 fusion.127
  533.6 7.6 fusion.128
  541.3 3.5 copy.26
  554.1 3.2 fusion.127
  566.5 7.6 fusion.128
  574.1 3.5 copy.26
  586.9 3.2 fusion.127
  599.3 7.6 fusion.128
  607.0 3.5 copy.26
  619.8 3.2 fusion.127
  632.2 7.6 fusion.128
  639.8 3.5 copy.26
  665.0 7.6 fusion.128
  672.7 3.5 copy.26
  685.5 3.2 fusion.127
  697.9 7.6 fusion.128
  705.5 3.5 copy.26
  712.6 85.6 %all-gather.2.cloned.1.call-done = f32[32,2,128,128]{3,2,1,0:T(8,128)} async-done(((f32[1,2,128,128]{3,2,1,0:T(8,128)}), f32[32,2,128,128]{3,2,1,0:T(8,128)}) %all-gather.2.cloned.1.call-update) | async-done | bytes 4194320 | tf_op jit(solution)/shard_map/all_gather | solution.py:132
  (128 shorter events, 119.6 us)
Async XLA Ops:
  6.5 38.2 %copy-start = (s32[1,1,2048,128]{3,2,1,0:T(8,128)S(1)}, s32[1,1,2048,128]{3,2,1,0:T(8,128)}, u32[]{:S(2)}) copy-start(s32[1,1,2048,128]{3,2,1,0:T(8,128)} %param.10) | copy-start | bytes 3145732
  23.0 18.1 %all-to-all-start = ((s32[16,192,1]{1,2,0:T(1,128)}), s32[16,192,1]{1,2,0:T(1,128)S(1)}, u32[]{:S(2)}, u32[]{:S(2)}) async-start(s32[16,192,1]{1,2,0:T(1,128)} %all_to_all.43), calls=%async_computation | async-start | bytes 32768 | tf_op jit(solution)/shard_map/all_to_all | solution.py:123
  41.1 30.3 %all-to-all-start.2 = ((bf16[16,64,512]{2,0,1:T(8,128)(2,1)}), bf16[16,64,512]{2,0,1:T(8,128)(2,1)S(1)}, u32[]{:S(2)}, u32[]{:S(2)}) async-start(bf16[16,64,512]{2,0,1:T(8,128)(2,1)} %copy.16), calls=%async_computation.2 | async-start | bytes 2097152 | tf_op jit(solution)/shard_map/all_to_all | solution.py:94
  71.3 199.0 %all-to-all-start.1 = ((s32[16,192,128]{2,1,0:T(8,128)}), s32[16,192,128]{2,1,0:T(8,128)}, u32[]{:S(2)}, u32[]{:S(2)}) async-start(s32[16,192,128]{2,1,0:T(8,128)} %bitcast.8), calls=%async_computation.1 | async-start | bytes 3145728 | tf_op jit(solution)/shard_map/all_to_all | solution.py:122
  82.5 233.5 %copy-start.1 = (bf16[2,8]{1,0:T(2,128)(2,1)S(1)}, bf16[2,8]{1,0:T(2,128)(2,1)}, u32[]{:S(2)}) copy-start(bf16[2,8]{1,0:T(2,128)(2,1)} %param.11) | copy-start | bytes 100
  270.3 45.7 %all-to-all-start.3 = ((bf16[3072,2,128]{2,1,0:T(2,128)(2,1)}), bf16[3072,2,128]{2,1,0:T(2,128)(2,1)}, u32[]{:S(2)}, u32[]{:S(2)}) async-start(bf16[3072,2,128]{2,1,0:T(2,128)(2,1)} %scatter_fusion), calls=%async_computation.3 | async-start | bytes 3145728 | tf_op jit(solution)/shard_map/all_to_all | solution.py:121
  278.1 520.1 %all-gather.2.cloned.1.call-start = ((), (), s32[]{:S(2)}) async-start(), calls=%async_computation.4 | async-start | bytes 4325376 | tf_op jit(solution)/shard_map/all_gather | solution.py:132
Sparse Core Ops, SparseCore 0:
  712.2 85.9 all-gather.1
